TPU v7x, 32 devices: a whole 2x2x4 slice. The times are simulated.
32 devices in a mesh: tm: 8 (over z, core), space: 4 (over y, x).
Axes of the slice: x: 2, y: 2, z: 4, core: 2. Of those that a mesh axis runs over, the one named last changes fastest.
Arguments:
- initial_temp: float32 [64, 32, 256], P('space'), may hold values from -6 to 6
- region_labels: int32 [16, 8, 64], P('space'), may hold values from 0 to 5
- region_rate: float32 [6], replicated, may hold values from 0.5 to 8
- heat_rate: float32 [8, 6], replicated, may hold values from 0.1 to 2
Outputs:
- slice_end: float32 [8, 64, 32, 256], P('tm', 'space')
All inputs are finite; a program needn't handle non-finite values.
Results may differ from a plain program's by a relative error of at most 0.0001.
Values sent between devices are 32-bit elements; how exact they have to be, the bound alone decides.
A program may use at most 128 MiB of HBM per device.

v0:
```python
import functools

import jax
import jax.numpy as jnp
from jax import lax
from jax.experimental import pallas as pl
from jax.experimental.pallas import tpu as pltpu
from jax.sharding import PartitionSpec as P

FINE_STEPS = 2
SWEEPS = 8
C_SWEEPS = 4
W1 = FINE_STEPS * SWEEPS
W2 = SWEEPS
F32 = jnp.float32
BF16 = jnp.bfloat16
MESH = pl.DeviceIdType.MESH
HI = lax.Precision.HIGHEST


def dot(a, b):
    return jnp.dot(a, b, precision=HI, preferred_element_type=F32)


def kernel(
    n_count, s_count,
    init_hbm, labels_hbm, rates_hbm, heat_hbm,
    out,
    raw, labels, rates, heat, in_sem, init,
    ag, gag, t0, u, sc, wt, inv, src, fs, fr, mid, kp, es, er, cs, cr, dcur,
    ag_ss, ag_rs, ih_ss, ih_rs, f_ss, f_rs, m_ss, m_rs, e_ss, e_rs, c_ss, c_rs,
):
    n = lax.axis_index("tm")
    s = lax.axis_index("space")
    planes, ny, nz = init_hbm.shape
    bx, cy, cz = labels_hbm.shape
    cx = bx * s_count
    lanes = ag.shape[-1]
    ts, zs = ny // cy, nz // lanes
    regions = rates_hbm.shape[1]
    pad = W1 // 4
    has_prev, has_next = n > 0, n < n_count - 1
    has_lo, has_hi = s > 0, s < s_count - 1

    pairs = [(labels_hbm, labels), (rates_hbm, rates), (heat_hbm, heat)]
    pairs += [(init_hbm.at[:, :, pl.ds(c * lanes, lanes)], raw.at[c]) for c in range(zs)]
    fetches = [pltpu.make_async_copy(a, b, in_sem.at[i]) for i, (a, b) in enumerate(pairs)]
    for fetch in fetches:
        fetch.start()

    barrier = pltpu.get_barrier_semaphore()
    def greet(cond, dev):
        @pl.when(cond)
        def _():
            pl.semaphore_signal(barrier, inc=1, device_id=dev, device_id_type=MESH)
    def one(c):
        return jnp.where(c, 1, 0).astype(jnp.int32)
    for j in range(1, s_count):
        pl.semaphore_signal(
            barrier, inc=1, device_id=(n, lax.rem(s + j, s_count)), device_id_type=MESH)
    partners = s_count - 1
    for cond_n, dn in ((has_prev, -1), (has_next, 1)):
        for cond_s, ds in ((None, 0), (has_lo, -1), (has_hi, 1)):
            cond = cond_n if cond_s is None else cond_n & cond_s
            greet(cond, (n + dn, s + ds))
            partners = partners + one(cond)
    pl.semaphore_wait(barrier, partners)

    def remote(a, b, ss, rs, dev):
        return pltpu.make_async_remote_copy(
            src_ref=a, dst_ref=b, send_sem=ss, recv_sem=rs, device_id=dev, device_id_type=MESH)

    half = 4 // zs

    def restrict(planes4):
        total = planes4[0]
        for extra in planes4[1:]:
            total = total + extra
        part = total[0]
        for k in range(1, ts * zs):
            part = part + total[k]
        lane = lax.broadcasted_iota(jnp.int32, part.shape, 1)
        step = 1
        while step < half:
            swap = jnp.where(lane % (2 * step) < step,
                             pltpu.roll(part, lanes - step, 1), pltpu.roll(part, step, 1))
            part = part + swap
            step *= 2
        return part * F32(1.0 / 64.0)

    def lookup(lab, row):
        total = jnp.zeros(lab.shape, F32)
        for r in range(regions):
            total = total + jnp.where(lab == F32(r), row(r), F32(0.0))
        return total

    crow = lax.broadcasted_iota(jnp.int32, (cx, cy, lanes), 1)
    ccol = lax.broadcasted_iota(jnp.int32, (cx, cy, lanes), 2)
    c_first, c_last = crow == 0, crow == cy - 1
    cz_first, cz_last = ccol < half, ccol >= lanes - half
    czero = jnp.zeros((1, cy, lanes), F32)

    def c_neighbours(w):
        total = jnp.concatenate([czero, w[:-1]], 0) + jnp.concatenate([w[1:], czero], 0)
        total = total + (jnp.where(c_first, F32(0.0), pltpu.roll(w, 1, 1))
                         + jnp.where(c_last, F32(0.0), pltpu.roll(w, cy - 1, 1)))
        return total + (jnp.where(cz_first, F32(0.0), pltpu.roll(w, half, 2))
                        + jnp.where(cz_last, F32(0.0), pltpu.roll(w, lanes - half, 2)))

    def c_jacobi(scaled, w, c_weight):
        for _ in range(C_SWEEPS):
            w = scaled + c_weight * c_neighbours(w)
        return w

    row = lax.broadcasted_iota(jnp.int32, (cy, lanes), 0)
    col = lax.broadcasted_iota(jnp.int32, (cy, lanes), 1)
    y_first, y_last = row == 0, row == cy - 1
    z_first, z_last = col == 0, col == lanes - 1

    def in_plane(w, k):
        t, c = k // zs, k % zs
        if t > 0:
            a = w[k - zs]
        else:
            a = jnp.where(y_first, F32(0.0), pltpu.roll(w[(ts - 1) * zs + c], 1, 0))
        if t < ts - 1:
            b = w[k + zs]
        else:
            b = jnp.where(y_last, F32(0.0), pltpu.roll(w[c], cy - 1, 0))
        if c > 0:
            d = w[k - 1]
        else:
            d = jnp.where(z_first, F32(0.0), pltpu.roll(w[k + zs - 1], 1, 1))
        if c < zs - 1:
            e = w[k + 1]
        else:
            e = jnp.where(z_last, F32(0.0), pltpu.roll(w[k - zs + 1], lanes - 1, 1))
        return (a + b) + (d + e)

    tiles = ts * zs

    def fine_step(first, length, shrink):
        def scale(q, _):
            g = first // 4 + q
            iv, so = inv[g], src[g]
            for r in range(4):
                p = first + 4 * q + r
                for k in range(tiles):
                    sc[p, k] = (u[p + 1, k] + so) * iv
            return 0
        lax.fori_loop(0, length // 4, scale, 0)

        def sweep(i, _):
            cut = 4 * (i // 4)
            lo = first + cut

            def quad(q, carry):
                before, cur = carry
                we = wt[lo // 4 + q]
                for r in range(4):
                    p = lo + 4 * q + r
                    after = [u[p + 2, k] for k in range(tiles)]
                    for k in range(tiles):
                        u[p + 1, k] = sc[p, k] + we * ((before[k] + after[k]) + in_plane(cur, k))
                    before, cur = cur, after
                return before, cur

            lax.fori_loop(0, (length - 2 * cut) // 4, quad,
                          ([u[lo, k] for k in range(tiles)], [u[lo + 1, k] for k in range(tiles)]))
            return 0
        lax.fori_loop(0, shrink, sweep, 0)

    def gather_start(stage, ref, mine):
        copies = []
        for j in range(1, s_count):
            copy = remote(mine(ref), mine(ref), ag_ss.at[stage, j], ag_rs.at[stage, j],
                          (n, lax.rem(s + j, s_count)))
            copy.start()
            copies.append(copy)
        return copies

    own = pl.ds(pad + bx * s, bx)

    ext = W1 * 2 + planes
    zero_block = jnp.zeros((pad, cy, lanes), F32)
    for k in (0, pad + cx):
        ag[0, k:k + pad] = zero_block
        ag[1, k:k + pad] = zero_block - 1.0
        kp[k:k + pad] = zero_block
    def zeros(*lead):
        return jnp.zeros(lead + (tiles, cy, lanes), F32)

    zero_fine = zeros()
    u[0] = zero_fine
    u[ext + 1] = zero_fine

    for fetch in fetches:
        fetch.wait()

    zi = lax.broadcasted_iota(jnp.int32, (nz, nz), 0)
    zj = lax.broadcasted_iota(jnp.int32, (nz, nz), 1)
    to_tiles = jnp.where(zi == zs * (zj % lanes) + zj // lanes, F32(1.0), F32(0.0)).astype(BF16)
    from_tiles = jnp.where(zj == zs * (zi % lanes) + zi // lanes, F32(1.0), F32(0.0)).astype(BF16)

    def permute(rows, one_hot):
        high = rows.astype(BF16)
        rest = rows - high.astype(F32)
        middle = rest.astype(BF16)
        low = (rest - middle.astype(F32)).astype(BF16)
        parts = [jnp.dot(x, one_hot, preferred_element_type=F32) for x in (high, middle, low)]
        return (parts[0] + parts[1]) + parts[2]

    def load(q, _):
        rows = jnp.concatenate([
            jnp.concatenate([raw[c, 4 * q + r, pl.ds(t, cy, stride=ts), :] for c in range(zs)], 1)
            for r in range(4) for t in range(ts)], 0)
        moved = permute(rows, to_tiles)
        for r in range(4):
            for t in range(ts):
                for c in range(zs):
                    at = (r * ts + t) * cy
                    init[4 * q + r, t * zs + c] = moved[at:at + cy, c * lanes:(c + 1) * lanes]
        return 0
    lax.fori_loop(0, bx, load, 0)

    li = lax.broadcasted_iota(jnp.int32, (cz, lanes), 0)
    lj = lax.broadcasted_iota(jnp.int32, (cz, lanes), 1)
    spread = jnp.where(li == lj // half, F32(1.0), F32(0.0))
    for k in range(bx):
        ag[0, pad + bx * s + k] = restrict([init[4 * k + r] for r in range(4)])
        ag[1, pad + bx * s + k] = dot(labels[k].astype(F32), spread)
    g0 = gather_start(0, ag, lambda r: r.at[:, own])

    first_slice = n == 0
    ih_lo = remote(init, t0.at[pl.ds(W1 + planes, W1)], ih_ss.at[0], ih_rs.at[0], (n, s - 1))
    ih_hi = remote(init, t0.at[pl.ds(0, W1)], ih_ss.at[1], ih_rs.at[1], (n, s + 1))

    @pl.when(first_slice & has_lo)
    def _():
        ih_lo.start()

    @pl.when(first_slice & has_hi)
    def _():
        ih_hi.start()

    @pl.when(jnp.logical_not(has_lo))
    def _():
        t0[0:W1] = zeros(W1)
        fr[0:W2] = zeros(W2)
        mid[0] = zeros(W2)

    @pl.when(jnp.logical_not(has_hi))
    def _():
        t0[W1 + planes:] = zeros(W1)
        fr[W2 + planes:] = zeros(W2)
        mid[1] = zeros(W2)

    for copy in g0:
        copy.wait()

    lab = ag[1, pl.ds(bx * s, ext // 4)]
    rate = lookup(lab, lambda r: rates[0, r])
    iv = 1.0 / (1.0 + 6.0 * rate)
    inv[...] = iv
    wt[...] = rate * iv
    src[...] = lookup(lab, lambda r: heat[n, r])

    lab_all = ag[1, pad:pad + cx]
    c_rate = FINE_STEPS * lookup(lab_all, lambda r: rates[0, r]) / 16.0
    c_inv = 1.0 / (1.0 + 6.0 * c_rate)
    c_weight = c_rate * c_inv

    def advance(m, c):
        source = FINE_STEPS * lookup(lab_all, lambda r: heat[m, r])
        return c_jacobi((c + source) * c_inv, c, c_weight)

    own_c = lax.fori_loop(0, n, advance, ag[0, pad:pad + cx])
    dcur[...] = advance(n, own_c)
    kp[pad:pad + cx] = own_c

    @pl.when(first_slice)
    def _():
        @pl.when(has_hi)
        def _():
            ih_lo_wait = remote(init, t0.at[pl.ds(W1 + planes, W1)], ih_ss.at[0], ih_rs.at[0], (n, s + 1))
            ih_lo_wait.wait_recv()

        @pl.when(has_lo)
        def _():
            ih_hi_wait = remote(init, t0.at[pl.ds(0, W1)], ih_ss.at[1], ih_rs.at[1], (n, s - 1))
            ih_hi_wait.wait_recv()

        def lay(p, _):
            u[1 + p] = t0[p]
            u[1 + W1 + planes + p] = t0[W1 + planes + p]
            return 0
        lax.fori_loop(0, W1, lay, 0)

        def lay_own(p, _):
            u[1 + W1 + p] = init[p]
            return 0
        lax.fori_loop(0, planes, lay_own, 0)

    @pl.when(has_prev)
    def _():
        def lay(k, _):
            f = kp[bx * s + k]
            for r in range(4):
                for q in range(tiles):
                    u[1 + 4 * k + r, q] = f
            return 0
        lax.fori_loop(0, ext // 4, lay, 0)

    fine_step(0, ext, SWEEPS)
    fine_step(SWEEPS, ext - 2 * SWEEPS, SWEEPS)

    own_g = pl.ds(bx * s, bx)

    def coarse_part(stage, plane_of):
        for k in range(bx):
            gag[stage, bx * s + k] = restrict([plane_of(4 * k + r) for r in range(4)])
        copies = gather_start(stage + 1, gag.at[stage], lambda r: r.at[own_g])
        return copies

    def keep(p, _):
        fs[p] = u[1 + W1 + p]
        return 0
    lax.fori_loop(0, planes, keep, 0)
    g1 = coarse_part(0, lambda p: fs[p])

    f_own = remote(fs, fr.at[pl.ds(W2, planes)], f_ss.at[0], f_rs.at[0], (n + 1, s))
    f_lo = remote(fs.at[pl.ds(0, W2)], fr.at[pl.ds(W2 + planes, W2)], f_ss.at[1], f_rs.at[1], (n + 1, s - 1))
    f_hi = remote(fs.at[pl.ds(planes - W2, W2)], fr.at[pl.ds(0, W2)], f_ss.at[2], f_rs.at[2], (n + 1, s + 1))

    @pl.when(has_next)
    def _():
        f_own.start()

    @pl.when(has_next & has_lo)
    def _():
        f_lo.start()

    @pl.when(has_next & has_hi)
    def _():
        f_hi.start()

    for copy in g1:
        copy.wait()

    def chain(stage):
        e_copy = remote(es.at[stage], er.at[stage], e_ss.at[stage], e_rs.at[stage], (n + 1, s))

        @pl.when(first_slice)
        def _():
            er[stage] = jnp.zeros((cx, cy, lanes), F32)

        @pl.when(has_prev)
        def _():
            e_copy.wait_recv()
        e = er[stage]
        corr = c_jacobi(e * c_inv, e, c_weight)
        rf = gag[stage]
        es[stage] = corr + (rf - dcur[...])

        @pl.when(has_next)
        def _():
            e_copy.start()
        dcur[...] = rf + corr
        return corr

    cs[...] = chain(0)
    c_copy = remote(cs, cr, c_ss, c_rs, (n + 1, s))

    @pl.when(has_next)
    def _():
        c_copy.start()

    off = W1 - W2
    span = planes + 2 * W2

    @pl.when(first_slice)
    def _():
        def lay(p, _):
            u[1 + off + p] = t0[off + p]
            u[1 + W1 + planes + p] = t0[W1 + planes + p]
            return 0
        lax.fori_loop(0, W2, lay, 0)

        def lay_own(p, _):
            u[1 + W1 + p] = init[p]
            return 0
        lax.fori_loop(0, planes, lay_own, 0)

    @pl.when(has_prev)
    def _():
        c_copy.wait_recv()
        f_own.wait_recv()

        @pl.when(has_hi)
        def _():
            f_lo.wait_recv()

        @pl.when(has_lo)
        def _():
            f_hi.wait_recv()
        kp[pad:pad + cx] = cr[...]

        def lay(k, _):
            f = kp[bx * s + off // 4 + k]
            for r in range(4):
                for q in range(tiles):
                    u[1 + off + 4 * k + r, q] = fr[4 * k + r, q] + f
            return 0
        lax.fori_loop(0, span // 4, lay, 0)

    fine_step(off, span, SWEEPS)

    m_lo = remote(u.at[pl.ds(1 + W1, W2)], mid.at[1], m_ss.at[0], m_rs.at[0], (n, s - 1))
    m_hi = remote(u.at[pl.ds(1 + W1 + planes - W2, W2)], mid.at[0], m_ss.at[1], m_rs.at[1], (n, s + 1))

    @pl.when(has_lo)
    def _():
        m_lo.start()

    @pl.when(has_hi)
    def _():
        m_hi.start()

    @pl.when(has_lo)
    def _():
        m_hi.wait_recv()
        m_lo.wait_send()

    @pl.when(has_hi)
    def _():
        m_lo.wait_recv()
        m_hi.wait_send()

    def lay_mid(p, _):
        u[1 + off + p] = mid[0, p]
        u[1 + W1 + planes + p] = mid[1, p]
        return 0
    lax.fori_loop(0, W2, lay_mid, 0)
    fine_step(off, span, SWEEPS)

    g2 = coarse_part(1, lambda p: u[1 + W1 + p])
    for copy in g2:
        copy.wait()
    kp[pad:pad + cx] = chain(1)

    def finish(q, _):
        f = kp[pad + bx * s + q]
        rows = jnp.concatenate([
            jnp.concatenate([u[1 + W1 + 4 * q + r, t * zs + c] + f for c in range(zs)], 1)
            for r in range(4) for t in range(ts)], 0)
        moved = permute(rows, from_tiles)
        for r in range(4):
            for t in range(ts):
                for c in range(zs):
                    at = (r * ts + t) * cy
                    raw[c, 4 * q + r, pl.ds(t, cy, stride=ts), :] = moved[at:at + cy, c * lanes:(c + 1) * lanes]
        return 0
    lax.fori_loop(0, bx, finish, 0)
    stores = [pltpu.make_async_copy(raw.at[c], out.at[0, :, :, pl.ds(c * lanes, lanes)], in_sem.at[c])
              for c in range(zs)]
    for store in stores:
        store.start()

    @pl.when(first_slice & has_lo)
    def _():
        ih_lo.wait_send()

    @pl.when(first_slice & has_hi)
    def _():
        ih_hi.wait_send()

    @pl.when(has_next)
    def _():
        f_own.wait_send()
        c_copy.wait_send()
        for stage in range(2):
            remote(es.at[stage], er.at[stage], e_ss.at[stage], e_rs.at[stage], (n + 1, s)).wait_send()

    @pl.when(has_next & has_lo)
    def _():
        f_lo.wait_send()

    @pl.when(has_next & has_hi)
    def _():
        f_hi.wait_send()

    for store in stores:
        store.wait()


def solution(mesh):
    n_count, s_count = mesh.shape["tm"], mesh.shape["space"]

    def on_device(init, labels, rates, heat):
        planes, ny, nz = init.shape
        bx, cy, cz = labels.shape
        cx = bx * s_count
        lanes = 128
        tile = (ny * nz // (cy * lanes), cy, lanes)
        pad = W1 // 4
        ext = planes + 2 * W1
        dma = pltpu.SemaphoreType.DMA

        def vm(*shape):
            return pltpu.VMEM(shape, F32)

        return pl.pallas_call(
            functools.partial(kernel, n_count, s_count),
            out_shape=jax.ShapeDtypeStruct((1, planes, ny, nz), F32),
            in_specs=[pl.BlockSpec(memory_space=pl.ANY)] * 4,
            out_specs=pl.BlockSpec(memory_space=pl.ANY),
            scratch_shapes=[
                vm(nz // lanes, planes, ny, lanes), pltpu.VMEM(labels.shape, labels.dtype),
                pltpu.SMEM((1, rates.shape[0]), F32), pltpu.SMEM(heat.shape, F32),
                dma((3 + nz // lanes,)), vm(planes, *tile),
                vm(2, cx + 2 * pad, cy, lanes),
                vm(2, cx, cy, lanes),
                vm(ext, *tile),
                vm(ext + 2, *tile),
                vm(ext, *tile), vm(ext // 4, cy, lanes), vm(ext // 4, cy, lanes), vm(ext // 4, cy, lanes),
                vm(planes, *tile),
                vm(planes + 2 * W2, *tile),
                vm(2, W2, *tile),
                vm(cx + 2 * pad, cy, lanes),
                vm(2, cx, cy, lanes), vm(2, cx, cy, lanes),
                vm(cx, cy, lanes), vm(cx, cy, lanes), vm(cx, cy, lanes),
                dma((3, s_count)), dma((3, s_count)),
                dma((2,)), dma((2,)),
                dma((3,)), dma((3,)),
                dma((2,)), dma((2,)),
                dma((2,)), dma((2,)),
                dma(()), dma(()),
            ],
            compiler_params=pltpu.CompilerParams(
                collective_id=0, has_side_effects=True, vmem_limit_bytes=48 * 1024 * 1024),
            name="parareal",
        )(init, labels, rates.reshape(1, -1), heat)

    return jax.shard_map(
        on_device,
        mesh=mesh,
        in_specs=(P("space", None, None), P("space", None, None), P(), P()),
        out_specs=P("tm", "space", None, None),
        check_vma=False,
    )
```

profile of v0, /device:TPU:27, one launch (start us, length us, event | category | flops | bytes accessed | tf_op | source)
XLA Modules:
  0.0 88.0 jit_solution(4343214738998801754)
XLA Ops:
  0.0 0.0 copy-start.3
  0.0 0.7 copy-done.3
  0.7 0.0 copy-start
  0.7 1.0 %copy-done = f32[16,32,256]{2,1,0:T(8,128)S(1)} copy-done((f32[16,32,256]{2,1,0:T(8,128)S(1)}, f32[16,32,256]{2,1,0:T(8,128)}, u32[]{:S(2)}) %copy-start) | copy-done | bytes 524312
  1.7 0.0 copy-start.1
  1.7 0.7 copy-done.1
  2.4 0.0 copy-start.2
  2.4 0.7 copy-done.2
  3.1 84.1 %parareal.1 = f32[1,16,32,256]{3,2,1,0:T(8,128)S(1)} custom-call(f32[16,32,256]{2,1,0:T(8,128)S(1)} %copy-done, s32[4,8,64]{2,1,0:T(8,128)S(1)} %copy-done.1, f32[1,6]{1,0:T(1,128)S(1)} %bitcast.1, f32[8,6]{1,0:T(8,128)S(1)} %copy-done.2), custom_call_target="tpu_custom_call" | custom-call | tf_op jit(solution)/shard_map/parareal/pallas_call | solution.py:512
  87.2 0.8 copy.6
Async XLA Ops:
  0.0 0.7 copy-start.3
  0.7 1.0 %copy-start = (f32[16,32,256]{2,1,0:T(8,128)S(1)}, f32[16,32,256]{2,1,0:T(8,128)}, u32[]{:S(2)}) copy-start(f32[16,32,256]{2,1,0:T(8,128)} %init_hbm.1) | copy-start | bytes 1572868
  1.7 0.7 copy-start.1
  2.4 0.7 copy-start.2
where the time goes:
time: 88.3 us; the launch traced here: 88 us
  Pallas kernels  84.1 us (95%)
  local copies, waits for them, and re-layouts  3.89 us (4%)
    pallas_call x1, Pallas kernels, on_device(): pl.pallas_call(functools.partial(kernel, n_count, s_count), out_shape=jax...  84.1 us
    unnamed x9, local copies, waits for them, and re-layouts  3.89 us

commit v1 on v0

v1 whole, which is shorter than its diff:
```python
import functools

import jax
import jax.numpy as jnp
from jax import lax
from jax.experimental import pallas as pl
from jax.experimental.pallas import tpu as pltpu
from jax.sharding import PartitionSpec as P

FINE_STEPS = 2
SWEEPS = 8
C_SWEEPS = 4
W = FINE_STEPS * SWEEPS
COARSE = 4
F32 = jnp.float32
BF16 = jnp.bfloat16
MESH = pl.DeviceIdType.MESH
HI = lax.Precision.HIGHEST
UNROLL = 4
WIDE = 8

ROW = (16, 0, 8, 32)
ROWS = 40


def kernel(
    n_count, s_count,
    init_hbm, labels_hbm, rates_hbm, heat_hbm,
    out,
    raw, labels, rates, heat, in_sem,
    init, nbr, ag, m1, m2, cst, w1, dl, clin, llin, wtp, inv, src, u, v, sc,
    ag_ss, ag_rs, i_ss, i_rs, m1_ss, m1_rs, m2_ss, m2_rs,
):
    n = lax.axis_index("tm")
    s = lax.axis_index("space")
    planes, ny, nz = init_hbm.shape
    bx, cy, cz = labels_hbm.shape
    cx = bx * s_count
    cq = cx // 2
    lanes = 2 * cz
    zs = nz // lanes
    regions = rates_hbm.shape[1]
    half = planes // 2
    bh = bx // 2
    pad = 2 * W // COARSE
    inner = W + half
    outer = W
    every = outer + inner
    has_prev = n > 0

    pairs = [(labels_hbm, labels), (rates_hbm, rates), (heat_hbm, heat)]
    pairs += [(init_hbm.at[:, :, pl.ds(c * lanes, lanes)], raw.at[c]) for c in range(zs)]
    fetches = [pltpu.make_async_copy(a, b, in_sem.at[i]) for i, (a, b) in enumerate(pairs)]
    for fetch in fetches:
        fetch.start()

    total = n_count * s_count
    barrier = pltpu.get_barrier_semaphore()

    def greet(k, _):
        other = lax.rem(n * s_count + s + k, total)
        pl.semaphore_signal(
            barrier, inc=1, device_id=(other // s_count, lax.rem(other, s_count)), device_id_type=MESH)
        return 0
    lax.fori_loop(1, total, greet, 0)

    def remote(a, b, ss, rs, dev):
        return pltpu.make_async_remote_copy(
            src_ref=a, dst_ref=b, send_sem=ss, recv_sem=rs, device_id=dev, device_id_type=MESH)

    lane = lax.broadcasted_iota(jnp.int32, (cy, lanes), 1)
    h0 = lane < cz
    z_first, z_last = lane % cz == 0, lane % cz == cz - 1
    zero = jnp.zeros((cy, lanes), F32)

    def swap(x):
        return pltpu.roll(x, cz, x.ndim - 1)

    def rows(t):
        return slice(ROW[t], ROW[t] + cy)

    def packed(t):
        return slice(t * cy, (t + 1) * cy)

    def clear_v(i, _):
        for k in range(outer + 2):
            for c in range(4):
                v[i, k, c, 24:32] = zero
        return 0
    lax.fori_loop(0, W + 1, clear_v, 0)

    def clear_u(k, _):
        for i in range(2):
            for c in range(4):
                u[i, k, c, 24:32] = zero
        return 0
    lax.fori_loop(0, inner + 2, clear_u, 0)
    for i in range(2):
        for c in range(4):
            for t in range(4):
                u[i, 0, c, rows(t)] = zero
    for k in range(pad):
        for at in (k, pad + cx + k):
            clin[at] = zero
            llin[at] = zero - 1.0

    zi = lax.broadcasted_iota(jnp.int32, (nz, nz), 0)
    zj = lax.broadcasted_iota(jnp.int32, (nz, nz), 1)
    to_tiles = jnp.where(zi == 4 * (zj % cz) + zj // cz, F32(1.0), F32(0.0)).astype(BF16)
    from_tiles = jnp.where(zj == 4 * (zi % cz) + zi // cz, F32(1.0), F32(0.0)).astype(BF16)

    def permute(x, one_hot):
        high = x.astype(BF16)
        rest = x - high.astype(F32)
        middle = rest.astype(BF16)
        low = (rest - middle.astype(F32)).astype(BF16)
        parts = [jnp.dot(y, one_hot, preferred_element_type=F32) for y in (high, middle, low)]
        return (parts[0] + parts[1]) + parts[2]

    for fetch in fetches:
        fetch.wait()

    def load(q, _):
        x = jnp.concatenate([
            jnp.concatenate([raw[c, plane, pl.ds(t, cy, stride=4), :] for c in range(zs)], 1)
            for r in range(2) for plane in (2 * q + r, planes - 1 - 2 * q - r) for t in range(4)], 0)
        moved = permute(x, to_tiles)
        for r in range(2):
            for t in range(4):
                for e in range(zs):
                    a = (r * 8 + t) * cy
                    b = (r * 8 + 4 + t) * cy
                    ta = moved[a:a + cy, e * lanes:(e + 1) * lanes]
                    tb = moved[b:b + cy, e * lanes:(e + 1) * lanes]
                    init[2 * q + r, 2 * e, packed(t)] = jnp.where(h0, ta, swap(tb))
                    init[2 * q + r, 2 * e + 1, packed(t)] = jnp.where(h0, swap(ta), tb)
        return 0
    lax.fori_loop(0, half // 2, load, 0)

    def restrict(tile):
        sums = []
        for q in range(bh):
            parts = [tile(COARSE * q + r, c, t) for r in range(COARSE) for c in range(4) for t in range(4)]
            while len(parts) > 1:
                parts = [a + b for a, b in zip(parts[::2], parts[1::2])]
            sums.append(parts[0] * F32(1.0 / 64.0))
        return sums

    li = lax.broadcasted_iota(jnp.int32, (cz, lanes), 0)
    lj = lax.broadcasted_iota(jnp.int32, (cz, lanes), 1)
    spread = [jnp.where(li == lj - h * cz, F32(1.0), F32(0.0)) for h in range(2)]
    means = restrict(lambda p, c, t: init[p, c, packed(t)])
    for q in range(bh):
        ag[s, q] = means[q]
        near = labels[q].astype(F32)
        far = labels[bx - 1 - q].astype(F32)
        ag[s, bh + q] = (jnp.dot(near, spread[0], precision=HI, preferred_element_type=F32)
                         + jnp.dot(far, spread[1], precision=HI, preferred_element_type=F32))

    pl.semaphore_wait(barrier, total - 1)

    gather = []
    for j in range(1, s_count):
        copy = remote(ag.at[s], ag.at[s], ag_ss.at[j], ag_rs.at[j], (n, lax.rem(s + j, s_count)))
        copy.start()
        gather.append(copy)

    aside = min(3, n_count - 1)
    has_lo, has_hi = s > 0, s < s_count - 1

    def to_even(c):
        return c & (lax.rem(s, 2) == 0)

    def to_odd(c):
        return c & (lax.rem(s, 2) == 1)
    routes = [
        (0, 1, 2, (n == 0) & (s < s_count - 2)),
        (3, 1, -2, (n == 0) & (s > 1)),
        (1, 0, 1, to_even((n == 1) & has_hi)),
        (2, 0, -1, to_odd((n == 1) & has_lo)),
        (1, 1 - aside, 1, to_odd((n == aside) & has_hi)),
        (2, 1 - aside, -1, to_even((n == aside) & has_lo)),
    ]
    spreads = [(cond, remote(init, nbr.at[slot], i_ss.at[k], i_rs.at[slot], (n + dn, s + ds)))
               for k, (slot, dn, ds, cond) in enumerate(routes)]
    for cond, copy in spreads:
        @pl.when(cond)
        def _(copy=copy):
            copy.start()
    there = [s > 1, has_lo, has_hi, s < s_count - 2]
    passed = [remote(nbr.at[slot], nbr.at[slot], i_ss.at[6 + k], i_rs.at[slot], (n - 1, s))
              for k, slot in enumerate((1, 2))]

    for slot in range(4):
        @pl.when((n <= 1) & jnp.logical_not(there[slot]))
        def _(slot=slot):
            def wipe(p, _):
                for c in range(4):
                    for t in range(4):
                        nbr[slot, p, c, packed(t)] = zero
                return 0
            lax.fori_loop(0, half, wipe, 0)

    for copy in gather:
        copy.wait()

    def spread_out(block):
        parts = []
        for q in range(cq):
            b, r = q // bx, q % bx
            if r < bh:
                parts.append(jnp.where(h0, block(b, r), block(s_count - 1 - b, r)))
            else:
                at = bx - 1 - r
                parts.append(swap(jnp.where(h0, block(s_count - 1 - b, at), block(b, at))))
        return jnp.stack(parts, 0)

    def to_line(ref, g):
        for q in range(cq):
            x, y = g[q], swap(g[q])
            ref[pad + q] = jnp.where(h0, x, y)
            ref[pad + cx - 1 - q] = jnp.where(h0, y, x)

    def local(ref, q):
        return jnp.where(h0, ref[bx * s + q], ref[bx * s + bx + 2 * pad - 1 - q])

    def lookup(lab, row):
        value = jnp.zeros(lab.shape, F32)
        for r in range(regions):
            value = value + jnp.where(lab == F32(r), row(r), F32(0.0))
        return value

    crow = lax.broadcasted_iota(jnp.int32, (cq, cy, lanes), 1)
    ccol = lax.broadcasted_iota(jnp.int32, (cq, cy, lanes), 2)
    c_first, c_last = crow == 0, crow == cy - 1
    cz_first, cz_last = ccol % cz == 0, ccol % cz == cz - 1
    czero = jnp.zeros((1, cy, lanes), F32)

    def c_neighbours(x):
        value = (jnp.concatenate([czero, x[:-1]], 0)
                 + jnp.concatenate([x[1:], swap(x[-1:])], 0))
        value = value + (jnp.where(c_first, F32(0.0), pltpu.roll(x, 1, 1))
                         + jnp.where(c_last, F32(0.0), pltpu.roll(x, cy - 1, 1)))
        return value + (jnp.where(cz_first, F32(0.0), pltpu.roll(x, 1, 2))
                        + jnp.where(cz_last, F32(0.0), pltpu.roll(x, lanes - 1, 2)))

    lab_all = spread_out(lambda b, r: ag[b, bh + r])
    c_rate = FINE_STEPS * lookup(lab_all, lambda r: rates[0, r]) / 16.0
    c_inv = 1.0 / (1.0 + 6.0 * c_rate)
    c_weight = c_rate * c_inv

    def c_jacobi(scaled, x):
        for _ in range(C_SWEEPS):
            x = scaled + c_weight * c_neighbours(x)
        return x

    cst[0] = spread_out(lambda b, r: ag[b, r])

    def advance(m, c):
        source = FINE_STEPS * lookup(lab_all, lambda r: heat[m, r])
        c = c_jacobi((c + source) * c_inv, c)
        cst[m + 1] = c
        return c

    to_line(llin, lab_all)

    @pl.when(n > 1)
    def _():
        to_line(clin, lax.fori_loop(0, n - 1, advance, cst[0]))
    slice_of_a = n - jnp.where(has_prev, 1, 0).astype(jnp.int32)

    for q in range(every // COARSE):
        lab = local(llin, q)
        rate = lookup(lab, lambda r: rates[0, r])
        iv = 1.0 / (1.0 + 6.0 * rate)
        inv[q] = iv
        src[q] = lookup(lab, lambda r: heat[slice_of_a, r])
        for r in range(COARSE):
            wtp[COARSE * q + r] = rate * iv

    def update(ref, level, k, p, step, put):
        def get(at, t, c):
            return ref[level, at, c, rows(t)]
        below, here, above = k, k + 1, k + 2
        g = [[ref[level, here, c, ROW[3] - 1:ROW[3] - 1 + cy] for c in range(4)]]
        g += [[get(here, t, c) for c in range(4)] for t in range(4)]
        g += [[ref[level, here, c, ROW[0] + 1:ROW[0] + 1 + cy] for c in range(4)]]
        for t in range(4):
            g[t + 1].append(jnp.where(z_last, F32(0.0), pltpu.roll(g[t + 1][0], lanes - 1, 1)))
        d = [[g[a + 1][b + 1] + g[a + 2][b] if a >= 0 or b < 3 else None for b in range(4)] for a in range(-1, 4)]
        left = [g[a + 1][0] + jnp.where(z_first, F32(0.0), pltpu.roll(g[a + 2][3], 1, 1)) for a in range(-1, 3)]
        we = wtp[p]
        for t in range(4):
            for c in range(4):
                around = d[t + 1][c] + (left[t] if c == 0 else d[t][c - 1])
                around = around + (get(below, t, c) + get(above, t, c))
                put(c, t, sc[step, p, c, packed(t)] + we * around)

    def scale(step, first, p0, count, plane):
        def quad(q, _):
            iv, so = inv[p0 // COARSE + q], src[p0 // COARSE + q]
            for r in range(COARSE):
                for c in range(4):
                    for t in range(4):
                        sc[step, p0 + COARSE * q + r, c, packed(t)] = (plane(COARSE * q + r, c, t) + so) * iv
            return 0
        lax.fori_loop(first, count // COARSE, quad, 0)

    quads = inner // UNROLL

    def solve_inner():
        def fine_step(step, _):
            scale(step, SWEEPS // COARSE * step, outer, inner, lambda p, c, t: u[0, 1 + p, c, rows(t)])

            def sweep(i, now):
                then = 1 - now

                def quad(q, edge):
                    for r in range(UNROLL):
                        p = UNROLL * q + r

                        def put(c, t, value, p=p, r=r):
                            u[then, 1 + p, c, rows(t)] = value
                            if edge and r == UNROLL - 1:
                                u[then, 2 + p, c, rows(t)] = swap(value)
                        update(u, now, p, outer + p, step, put)
                    return 0
                lax.fori_loop((1 + i) // UNROLL, quads - 1, lambda q, _: quad(q, False), 0)
                quad(quads - 1, True)
                for e in range(2):
                    for c in range(4):
                        for t in range(4):
                            v[i + 1, outer + e, c, rows(t)] = u[then, 2 + i + e, c, rows(t)]

            def two(j, _):
                sweep(SWEEPS * step + 2 * j, 0)
                sweep(SWEEPS * step + 2 * j + 1, 1)
                return 0
            lax.fori_loop(0, SWEEPS // 2, two, 0)
            return 0
        lax.fori_loop(0, FINE_STEPS, fine_step, 0)

    def solve_outer():
        def fine_step(step, _):
            p0 = SWEEPS * step
            scale(step, 0, p0, outer, lambda k, c, t: v[p0, k, c, rows(t)])

            def sweep(i, _):
                def part(q, _):
                    for r in range(WIDE):
                        k = WIDE * q + r

                        def put(c, t, value, k=k):
                            v[i + 1, k, c, rows(t)] = value
                        update(v, i, k, i + 1 + k, step, put)
                    return 0
                lax.fori_loop(0, outer // WIDE, part, 0)
                return 0
            lax.fori_loop(SWEEPS * step, SWEEPS * (step + 1), sweep, 0)
            return 0
        lax.fori_loop(0, FINE_STEPS, fine_step, 0)

    def mirror():
        for c in range(4):
            for t in range(4):
                u[0, 1 + inner, c, rows(t)] = swap(u[0, inner, c, rows(t)])

    def around_block(low, high, put):
        def near(x, _):
            for c in range(4):
                for t in range(4):
                    put(x, c, t, jnp.where(h0, nbr[low, x, c, packed(t)], nbr[high, x, c, packed(t)]))
                    put(planes - 1 - x, c, t, swap(
                        jnp.where(h0, nbr[high, x, c, packed(t)], nbr[low, x, c, packed(t)])))
            return 0
        lax.fori_loop(0, half, near, 0)

    def put_u(p, c, t, value):
        u[0, 1 + p, c, rows(t)] = value

    def put_v(p, c, t, value):
        v[0, p, c, rows(t)] = value

    def arrived(slot):
        remote(init, nbr.at[slot], i_ss.at[0], i_rs.at[slot], (n + 1, s)).wait_recv()

    @pl.when(n <= 1)
    def _():
        for slot in (1, 2):
            @pl.when(there[slot])
            def _(slot=slot):
                arrived(slot)
                @pl.when(n == 1)
                def _():
                    passed[slot - 1].start()
        around_block(1, 2, put_u)

        def own(p, _):
            for c in range(4):
                for t in range(4):
                    u[0, 1 + W + p, c, rows(t)] = init[p, c, packed(t)]
            return 0
        lax.fori_loop(0, half, own, 0)

    @pl.when(n > 1)
    def _():
        def own(q, _):
            f = local(clin, outer // COARSE + q)
            for r in range(COARSE):
                for c in range(4):
                    for t in range(4):
                        u[0, 1 + COARSE * q + r, c, rows(t)] = f
            return 0
        lax.fori_loop(0, inner // COARSE, own, 0)

        def far(q, _):
            f = local(clin, q)
            for r in range(COARSE):
                for c in range(4):
                    for t in range(4):
                        v[0, COARSE * q + r, c, rows(t)] = f
            return 0
        lax.fori_loop(0, outer // COARSE, far, 0)

    mirror()
    for e in range(2):
        for c in range(4):
            for t in range(4):
                v[0, outer + e, c, rows(t)] = u[0, 1 + e, c, rows(t)]
    solve_inner()

    def later(box, ss, rs, d0):
        for d in range(n_count - 1, d0 - 1, -1):
            for j in range(s_count):
                if d + j > 0:
                    yield n + d < n_count, remote(
                        box.at[n, s], box.at[n, s], ss.at[d, j], rs.at[d, j], (n + d, lax.rem(s + j, s_count)))

    def share(box, ss, rs, d0):
        means = restrict(lambda p, c, t: u[0, 1 + W + p, c, rows(t)])
        for q in range(bh):
            box[n, s, q] = means[q]
        for cond, copy in later(box, ss, rs, d0):
            @pl.when(cond)
            def _(copy=copy):
                copy.start()

    def drain(box, ss, rs, d0):
        for cond, copy in later(box, ss, rs, d0):
            @pl.when(cond)
            def _(copy=copy):
                copy.wait_send()

    def collect(box, ss, rs, distances):
        for d in distances:
            @pl.when(n - d >= 1)
            def _(d=d):
                for j in range(s_count):
                    if d + j > 0:
                        b = lax.rem(s + s_count - j, s_count)
                        remote(box.at[n - d, b], box.at[n - d, b], ss.at[d, j], rs.at[d, j], (n - d, b)).wait_recv()

    def whole(box, m):
        return spread_out(lambda b, r: box[m, b, r])

    c_shape = (cq, cy, lanes)

    @pl.when(has_prev)
    def _():
        share(m1, m1_ss, m1_rs, 0)

        @pl.when(n == 1)
        def _():
            for slot in (0, 3):
                @pl.when(there[slot])
                def _(slot=slot):
                    arrived(slot)
            around_block(0, 3, put_v)
        solve_outer()

        def correct(m, e):
            delta = c_jacobi(e * c_inv, e)
            rf = whole(m1, m + 1)
            w1[m] = rf + delta
            return delta + (rf - cst[m + 1])
        collect(m1, m1_ss, m1_rs, range(n_count - 1, 0, -1))
        e = lax.fori_loop(0, n - 1, correct, jnp.zeros(c_shape, F32))
        delta = c_jacobi(e * c_inv, e)
        dl[...] = delta
        to_line(clin, delta)

        for q in range(inner // COARSE):
            at = outer // COARSE + q
            src[at] = lookup(local(llin, at), lambda r: heat[n, r])

        def start(q, _):
            f = local(clin, outer // COARSE + q)
            for r in range(COARSE):
                for c in range(4):
                    for t in range(4):
                        u[0, 1 + COARSE * q + r, c, rows(t)] = v[W, COARSE * q + r, c, rows(t)] + f
            return 0
        lax.fori_loop(0, W // COARSE, start, 0)

        def start_own(q, _):
            f = local(clin, (outer + W) // COARSE + q)
            for r in range(COARSE):
                for c in range(4):
                    for t in range(4):
                        at = 1 + W + COARSE * q + r
                        u[0, at, c, rows(t)] = u[0, at, c, rows(t)] + f
            return 0
        lax.fori_loop(0, half // COARSE, start_own, 0)
        mirror()
        solve_inner()
        share(m2, m2_ss, m2_rs, 1)

        collect(m1, m1_ss, m1_rs, [0])
        w1[n - 1] = whole(m1, n) + dl[...]
        collect(m2, m2_ss, m2_rs, range(n_count - 1, 0, -1))

        def again(m, e):
            delta = c_jacobi(e * c_inv, e)
            rf = whole(m2, m)
            return delta + (rf - w1[m])
        e = lax.fori_loop(1, n, again, jnp.zeros(c_shape, F32))
        to_line(clin, c_jacobi(e * c_inv, e))

    @pl.when(jnp.logical_not(has_prev))
    def _():
        to_line(clin, jnp.zeros(c_shape, F32))

    def finish(q, _):
        parts = []
        f = local(clin, (outer + W) // COARSE + q // 2)
        for r in range(2):
            tiles = [[u[0, 1 + W + 2 * q + r, c, rows(t)] + f for c in range(4)] for t in range(4)]
            for side in range(2):
                for t in range(4):
                    row = []
                    for e in range(zs):
                        x, y = tiles[t][2 * e], tiles[t][2 * e + 1]
                        row.append(jnp.where(h0, x, swap(y)) if side == 0 else jnp.where(h0, swap(x), y))
                    parts.append(jnp.concatenate(row, 1))
        moved = permute(jnp.concatenate(parts, 0), from_tiles)
        for r in range(2):
            for side, plane in enumerate((2 * q + r, planes - 1 - 2 * q - r)):
                for t in range(4):
                    at = (r * 8 + side * 4 + t) * cy
                    for c in range(zs):
                        raw[c, plane, pl.ds(t, cy, stride=4), :] = moved[at:at + cy, c * lanes:(c + 1) * lanes]
        return 0
    lax.fori_loop(0, half // 2, finish, 0)
    stores = [pltpu.make_async_copy(raw.at[c], out.at[0, :, :, pl.ds(c * lanes, lanes)], in_sem.at[c])
              for c in range(zs)]
    for store in stores:
        store.start()

    for cond, copy in spreads:
        @pl.when(cond)
        def _(copy=copy):
            copy.wait_send()
    for slot in (1, 2):
        @pl.when((n == 1) & there[slot])
        def _(slot=slot):
            passed[slot - 1].wait_send()

    @pl.when(has_prev)
    def _():
        drain(m1, m1_ss, m1_rs, 0)
        drain(m2, m2_ss, m2_rs, 1)

    for store in stores:
        store.wait()


def solution(mesh):
    n_count, s_count = mesh.shape["tm"], mesh.shape["space"]

    def on_device(init, labels, rates, heat):
        planes, ny, nz = init.shape
        bx, cy, cz = labels.shape
        cx = bx * s_count
        lanes = 2 * cz
        zs = nz // lanes
        half, bh, cq = planes // 2, bx // 2, cx // 2
        pad = 2 * W // COARSE
        inner, every = W + half, 2 * W + half
        dma = pltpu.SemaphoreType.DMA

        def vm(*shape):
            return pltpu.VMEM(shape, F32)

        return pl.pallas_call(
            functools.partial(kernel, n_count, s_count),
            out_shape=jax.ShapeDtypeStruct((1, planes, ny, nz), F32),
            in_specs=[pl.BlockSpec(memory_space=pl.ANY)] * 4,
            out_specs=pl.BlockSpec(memory_space=pl.ANY),
            scratch_shapes=[
                vm(zs, planes, ny, lanes), pltpu.VMEM(labels.shape, labels.dtype),
                pltpu.SMEM((1, rates.shape[0]), F32), pltpu.SMEM(heat.shape, F32),
                dma((3 + zs,)),
                vm(half, 4, 4 * cy, lanes), vm(4, half, 4, 4 * cy, lanes),
                vm(s_count, 2 * bh, cy, lanes),
                vm(n_count, s_count, bh, cy, lanes), vm(n_count, s_count, bh, cy, lanes),
                vm(n_count, cq, cy, lanes), vm(n_count, cq, cy, lanes), vm(cq, cy, lanes),
                vm(cx + 2 * pad, cy, lanes), vm(cx + 2 * pad, cy, lanes),
                vm(every, cy, lanes), vm(every // COARSE, cy, lanes), vm(every // COARSE, cy, lanes),
                vm(2, inner + 2, 4, ROWS, lanes),
                vm(W + 1, W + 2, 4, ROWS, lanes),
                vm(2, every, 4, 4 * cy, lanes),
                dma((s_count,)), dma((s_count,)),
                dma((8,)), dma((4,)),
                dma((n_count, s_count)), dma((n_count, s_count)),
                dma((n_count, s_count)), dma((n_count, s_count)),
            ],
            compiler_params=pltpu.CompilerParams(
                collective_id=0, has_side_effects=True, vmem_limit_bytes=50 * 1024 * 1024),
            name="parareal",
        )(init, labels, rates.reshape(1, -1), heat)

    return jax.shard_map(
        on_device,
        mesh=mesh,
        in_specs=(P("space", None, None), P("space", None, None), P(), P()),
        out_specs=P("tm", "space", None, None),
        check_vma=False,
    )
```

time: 88.3 us -> 56.8 us (0.64)
  the two profiles are of different devices: /device:TPU:27 before, /device:TPU:16 now
where the time goes in v1:
time: 56.8 us; the launch traced here: 56.5 us
  Pallas kernels  52.6 us (93%)
  local copies, waits for them, and re-layouts  3.89 us (7%)
    pallas_call x1, Pallas kernels, on_device(): pl.pallas_call(functools.partial(kernel, n_count, s_count), out_shape=jax...  52.6 us
    unnamed x9, local copies, waits for them, and re-layouts  3.89 us

profile of v1, /device:TPU:16, one launch (start us, length us, event | category | flops | bytes accessed | tf_op | source)
XLA Modules:
  0.0 56.5 jit_solution(6536209997851542744)
XLA Ops:
  0.0 0.0 copy-start.3
  0.0 0.7 %copy-done.3 = f32[6]{0:T(128)S(1)} copy-done((f32[6]{0:T(128)S(1)}, f32[6]{0:T(128)}, u32[]{:S(2)}) %copy-start.3) | copy-done | bytes 48
  0.7 0.0 copy-start
  0.7 1.0 %copy-done = f32[16,32,256]{2,1,0:T(8,128)S(1)} copy-done((f32[16,32,256]{2,1,0:T(8,128)S(1)}, f32[16,32,256]{2,1,0:T(8,128)}, u32[]{:S(2)}) %copy-start) | copy-done | bytes 524312
  1.7 0.0 copy-start.1
  1.7 0.7 %copy-done.1 = s32[4,8,64]{2,1,0:T(8,128)S(1)} copy-done((s32[4,8,64]{2,1,0:T(8,128)S(1)}, s32[4,8,64]{2,1,0:T(8,128)}, u32[]{:S(2)}) %copy-start.1) | copy-done | bytes 8216
  2.4 0.0 copy-start.2
  2.4 0.7 %copy-done.2 = f32[8,6]{1,0:T(8,128)S(1)} copy-done((f32[8,6]{1,0:T(8,128)S(1)}, f32[8,6]{1,0:T(8,128)}, u32[]{:S(2)}) %copy-start.2) | copy-done | bytes 216
  3.1 52.6 %parareal.1 = f32[1,16,32,256]{3,2,1,0:T(8,128)S(1)} custom-call(f32[16,32,256]{2,1,0:T(8,128)S(1)} %copy-done, s32[4,8,64]{2,1,0:T(8,128)S(1)} %copy-done.1, f32[1,6]{1,0:T(1,128)S(1)} %bitcast.1, f32[8,6]{1,0:T(8,128)S(1)} %copy-done.2), custom_call_target="tpu_custom_call" | custom-call | tf_op jit(solution)/shard_map/parareal/pallas_call | solution.py:594
  55.7 0.8 %copy.6 = f32[1,16,32,256]{3,2,1,0:T(8,128)} copy(f32[1,16,32,256]{3,2,1,0:T(8,128)S(1)} %parareal.1) | data formatting | bytes 1048576
Async XLA Ops:
  0.0 0.7 %copy-start.3 = (f32[6]{0:T(128)S(1)}, f32[6]{0:T(128)}, u32[]{:S(2)}) copy-start(f32[6]{0:T(128)} %param.6) | copy-start | bytes 76
  0.7 1.0 %copy-start = (f32[16,32,256]{2,1,0:T(8,128)S(1)}, f32[16,32,256]{2,1,0:T(8,128)}, u32[]{:S(2)}) copy-start(f32[16,32,256]{2,1,0:T(8,128)} %init_hbm.1) | copy-start | bytes 1572868
  1.7 0.7 %copy-start.1 = (s32[4,8,64]{2,1,0:T(8,128)S(1)}, s32[4,8,64]{2,1,0:T(8,128)}, u32[]{:S(2)}) copy-start(s32[4,8,64]{2,1,0:T(8,128)} %labels_hbm.1) | copy-start | bytes 24580
  2.4 0.7 %copy-start.2 = (f32[8,6]{1,0:T(8,128)S(1)}, f32[8,6]{1,0:T(8,128)}, u32[]{:S(2)}) copy-start(f32[8,6]{1,0:T(8,128)} %heat_hbm.1) | copy-start | bytes 580

commit v2 on v1

--- a/solution.py
+++ b/solution.py
@@ -306,8 +306,6 @@
             return 0
         lax.fori_loop(first, count // COARSE, quad, 0)
 
-    quads = inner // UNROLL
-
     def solve_inner():
         def fine_step(step, _):
             scale(step, SWEEPS // COARSE * step, outer, inner, lambda p, c, t: u[0, 1 + p, c, rows(t)])
@@ -315,18 +313,20 @@
             def sweep(i, now):
                 then = 1 - now
 
-                def quad(q, edge):
-                    for r in range(UNROLL):
-                        p = UNROLL * q + r
+                def block(p0, count, edge):
+                    for r in range(count):
+                        p = p0 + r
 
                         def put(c, t, value, p=p, r=r):
                             u[then, 1 + p, c, rows(t)] = value
-                            if edge and r == UNROLL - 1:
+                            if edge and r == count - 1:
                                 u[then, 2 + p, c, rows(t)] = swap(value)
                         update(u, now, p, outer + p, step, put)
                     return 0
-                lax.fori_loop((1 + i) // UNROLL, quads - 1, lambda q, _: quad(q, False), 0)
-                quad(quads - 1, True)
+                first = (1 + i) // UNROLL
+                lax.fori_loop(first, first + lax.rem(first, 2), lambda q, _: block(UNROLL * q, UNROLL, False), 0)
+                lax.fori_loop((first + 1) // 2, inner // WIDE - 1, lambda q, _: block(WIDE * q, WIDE, False), 0)
+                block(inner - WIDE, WIDE, True)
                 for e in range(2):
                     for c in range(4):
                         for t in range(4):
@@ -515,9 +515,11 @@
         solve_inner()
         share(m2, m2_ss, m2_rs, 1)
 
+        drain(m1, m1_ss, m1_rs, 0)
         collect(m1, m1_ss, m1_rs, [0])
         w1[n - 1] = whole(m1, n) + dl[...]
         collect(m2, m2_ss, m2_rs, range(n_count - 1, 0, -1))
+        drain(m2, m2_ss, m2_rs, 1)
 
         def again(m, e):
             delta = c_jacobi(e * c_inv, e)
@@ -565,11 +567,6 @@
         def _(slot=slot):
             passed[slot - 1].wait_send()
 
-    @pl.when(has_prev)
-    def _():
-        drain(m1, m1_ss, m1_rs, 0)
-        drain(m2, m2_ss, m2_rs, 1)
-
     for store in stores:
         store.wait()
 
@@ -615,7 +612,7 @@
                 dma((n_count, s_count)), dma((n_count, s_count)),
             ],
             compiler_params=pltpu.CompilerParams(
-                collective_id=0, has_side_effects=True, vmem_limit_bytes=50 * 1024 * 1024),
+                collective_id=0, has_side_effects=True, vmem_limit_bytes=67_043_328),
             name="parareal",
         )(init, labels, rates.reshape(1, -1), heat)
 

time: 56.8 us -> 50.3 us (0.89)
  Pallas kernels: 52.6 us -> 48.2 us
  local copies, waits for them, and re-layouts: 3.89 us -> 1.88 us
    pallas_call x1, Pallas kernels: 52.6 us -> 48.2 us  [on_device(): pl.pallas_call(functools.partial(kernel, n_count, s_count), out_shape=jax...]
    unnamed x9 -> x1, local copies, waits for them, and re-layouts: 3.89 us -> 1.88 us
where the time goes in v2:
time: 50.3 us; the launch traced here: 50.1 us
  Pallas kernels  48.2 us (96%)
  local copies, waits for them, and re-layouts  1.88 us (4%)
    pallas_call x1, Pallas kernels, on_device(): pl.pallas_call(functools.partial(kernel, n_count, s_count), out_shape=jax...  48.2 us
    unnamed x1, local copies, waits for them, and re-layouts  1.88 us

profile of v2, /device:TPU:16, one launch (start us, length us, event | category | flops | bytes accessed | tf_op | source)
XLA Modules:
  0.0 50.1 jit_solution(14418470707534627624)
XLA Ops:
  0.0 48.2 %parareal.1 = f32[1,16,32,256]{3,2,1,0:T(8,128)} custom-call(f32[16,32,256]{2,1,0:T(8,128)} %init_hbm.1, s32[4,8,64]{2,1,0:T(8,128)} %labels_hbm.1, f32[1,6]{1,0:T(1,128)} %bitcast.1, f32[8,6]{1,0:T(8,128)} %heat_hbm.1), custom_call_target="tpu_custom_call" | custom-call | tf_op jit(solution)/shard_map/parareal/pallas_call | solution.py:591
  48.3 1.9 %copy.6 = f32[1,16,32,256]{3,2,1,0:T(8,128)} copy(f32[1,16,32,256]{3,2,1,0:T(8,128)} %parareal.1) | data formatting | bytes 1048576

commit v3 on v2

--- a/solution.py
+++ b/solution.py
@@ -518,14 +518,16 @@
         drain(m1, m1_ss, m1_rs, 0)
         collect(m1, m1_ss, m1_rs, [0])
         w1[n - 1] = whole(m1, n) + dl[...]
-        collect(m2, m2_ss, m2_rs, range(n_count - 1, 0, -1))
+        dl[...] = jnp.zeros(c_shape, F32)
+        for d in range(n_count - 1, 0, -1):
+            collect(m2, m2_ss, m2_rs, [d])
+
+            @pl.when(n - d >= 1)
+            def _(d=d):
+                e = dl[...]
+                dl[...] = c_jacobi(e * c_inv, e) + (whole(m2, n - d) - w1[n - d])
         drain(m2, m2_ss, m2_rs, 1)
-
-        def again(m, e):
-            delta = c_jacobi(e * c_inv, e)
-            rf = whole(m2, m)
-            return delta + (rf - w1[m])
-        e = lax.fori_loop(1, n, again, jnp.zeros(c_shape, F32))
+        e = dl[...]
         to_line(clin, c_jacobi(e * c_inv, e))
 
     @pl.when(jnp.logical_not(has_prev))

time: 50.3 us -> 50 us (level)
  no operation moved by 1% of the time
where the time goes in v3:
time: 50 us; the launch traced here: 49.8 us
  Pallas kernels  47.9 us (96%)
  local copies, waits for them, and re-layouts  1.88 us (4%)
    pallas_call x1, Pallas kernels, on_device(): pl.pallas_call(functools.partial(kernel, n_count, s_count), out_shape=jax...  47.9 us
    unnamed x1, local copies, waits for them, and re-layouts  1.88 us

profile of v3, /device:TPU:16, one launch (start us, length us, event | category | flops | bytes accessed | tf_op | source)
XLA Modules:
  0.0 49.8 jit_solution(13140452959924591815)
XLA Ops:
  0.0 47.9 %parareal.1 = f32[1,16,32,256]{3,2,1,0:T(8,128)} custom-call(f32[16,32,256]{2,1,0:T(8,128)} %init_hbm.1, s32[4,8,64]{2,1,0:T(8,128)} %labels_hbm.1, f32[1,6]{1,0:T(1,128)} %bitcast.1, f32[8,6]{1,0:T(8,128)} %heat_hbm.1), custom_call_target="tpu_custom_call" | custom-call | tf_op jit(solution)/shard_map/parareal/pallas_call | solution.py:593
  47.9 1.9 %copy.6 = f32[1,16,32,256]{3,2,1,0:T(8,128)} copy(f32[1,16,32,256]{3,2,1,0:T(8,128)} %parareal.1) | data formatting | bytes 1048576
